TPU v7x, 32 devices: a whole 2x2x4 slice. The times are simulated.
32 devices in a mesh: gx: 2 (over x), gy: 4 (over y, core), gz: 4 (over z).
Axes of the slice: x: 2, y: 2, z: 4, core: 2. Of those that a mesh axis runs over, the one named last changes fastest.
Arguments:
- t_matrix: float32 [1, 2, 4, 16, 1024], P(None, 'gx', 'gy', 'gz'), may hold values from -3 to 3
- structure: float32 [1, 1440, 1440], replicated, may hold values from -0.0390625 to 0.0390625
- species: int32 [2, 4, 16], P('gx', 'gy', 'gz'), may hold values from 0 to 3
- members: int32 [2, 4, 16, 45], P('gx', 'gy', 'gz'), may hold values from -1 to 44, as said below
- delta_table: float32 [4, 1024], replicated, may hold values from -4 to 4
Outputs:
- site_tau: float32 [1, 2, 4, 16, 1024], P(None, 'gx', 'gy', 'gz')
- pair_terms: float32 [2, 4, 16, 45], P('gx', 'gy', 'gz')
Inputs may be any that keep to these rules, and one draw needn't show every extreme that they name: `members`: each site's list names distinct window cells, the centre cell first, 27 to 45 of them, then -1 in the remaining slots; in every draw some site lists all 45 cells.
All inputs are finite; a program needn't handle non-finite values.
Results may differ from a plain program's by a relative error of at most 0.00013.
Values sent between devices are 32-bit elements; how exact they have to be, the bound alone decides.
No kernel may reach another device: no remote copies, remote signals or barrier semaphores. Data moves between devices by JAX's collectives and lax.ppermute only.
A program may use at most 192 MiB of HBM per device.

v0:
```python
import functools

import jax
import jax.numpy as jnp
import numpy as np
from jax import lax
from jax.experimental import pallas as pl
from jax.experimental.pallas import tpu as pltpu
from jax.sharding import PartitionSpec as P


L2 = 32
WINDOW = 45
ITERS = 4
SPECIES = 4
DEPTH = 4
LANES = DEPTH * L2
ROWS = WINDOW * L2
CENTRE = WINDOW // 2
SUM_ROWS = 48
PACK_ROWS = L2 + 8
PIECES = 1
PIECE = WINDOW // PIECES
PIECE_ROWS = PIECE * L2
SPLIT_STEPS = 9
CHUNK = 23
MESH_AXES = ("gx", "gy", "gz")


bf16 = jnp.bfloat16
f32 = jnp.float32
MIB = 1 << 20


def shifted(x, shift):
    sizes = [lax.axis_size(axis) for axis in MESH_AXES]
    pairs = []
    for source in np.ndindex(*sizes):
        target = [(i + d) % n for i, d, n in zip(source, shift, sizes)]
        pairs.append(
            (int(np.ravel_multi_index(source, sizes)), int(np.ravel_multi_index(target, sizes)))
        )
    return lax.ppermute(x, MESH_AXES, pairs)


def in_vmem(count):
    return [pl.BlockSpec(memory_space=pltpu.VMEM)] * count


def in_hbm(x):
    return pltpu.with_memory_space_constraint(x, pltpu.HBM)


def halves(x):
    high = x.astype(bf16)
    return high, (x - high.astype(f32)).astype(bf16)


def lane_index(shape):
    return lax.broadcasted_iota(jnp.int32, shape, len(shape) - 1)


def tile_kernel(flat_ref, tile_ref):
    row = lax.broadcasted_iota(jnp.int32, (DEPTH, LANES), 0)
    diagonal = lane_index((DEPTH, LANES)) // L2 == row
    for j in range(L2 // DEPTH):
        part = flat_ref[:, j * LANES : (j + 1) * LANES]
        rolled = [part] + [pltpu.roll(part, m * L2, 1) for m in range(1, DEPTH)]
        for k in range(DEPTH):
            picked = jnp.zeros((DEPTH, LANES), f32)
            for m in range(DEPTH):
                picked = jnp.where(diagonal & (row == (m + k) % DEPTH), rolled[m], picked)
            a = j * DEPTH + k
            tile_ref[a : a + 1, :] = jnp.sum(picked, axis=0, keepdims=True)


def flat_kernel(tile_ref, flat_ref):
    row = lax.broadcasted_iota(jnp.int32, (DEPTH, LANES), 0)
    diagonal = lane_index((DEPTH, LANES)) // L2 == row
    for j in range(L2 // DEPTH):
        spread = []
        for k in range(DEPTH):
            a = j * DEPTH + k
            line = jnp.broadcast_to(tile_ref[a : a + 1, :], (DEPTH, LANES))
            spread.append(jnp.where(diagonal, line, 0.0))
        value = jnp.zeros((DEPTH, LANES), f32)
        for m in range(DEPTH):
            picked = jnp.zeros((DEPTH, LANES), f32)
            for k in range(DEPTH):
                picked = jnp.where(row == (k - m) % DEPTH, spread[k], picked)
            value = value + (picked if m == 0 else pltpu.roll(picked, m * L2, 1))
        flat_ref[:, j * LANES : (j + 1) * LANES] = value


def pack_kernel(flat_hbm, members_hbm, species_hbm, pack_ref, flat_ref, members_ref, species_ref, sems):
    moves = [(flat_hbm, flat_ref), (members_hbm, members_ref), (species_hbm, species_ref)]
    copies = [
        pltpu.make_async_copy(source, target, sems.at[i])
        for i, (source, target) in enumerate(moves)
    ]
    for copy in copies:
        copy.start()
    for copy in copies:
        copy.wait()
    tile_kernel(flat_ref, pack_ref)
    pack_ref[L2:, :] = jnp.full((PACK_ROWS - L2, LANES), -1.0, f32)
    pack_ref[L2 : L2 + DEPTH, :WINDOW] = members_ref[...].astype(f32)
    pack_ref[L2 + DEPTH : L2 + DEPTH + 1, :DEPTH] = species_ref[...].astype(f32)


def packed_own(flat, members, species):
    return pl.pallas_call(
        pack_kernel,
        out_shape=jax.ShapeDtypeStruct((PACK_ROWS, LANES), f32),
        in_specs=[pl.BlockSpec(memory_space=pltpu.HBM)] * 3,
        out_specs=in_vmem(1)[0],
        scratch_shapes=[
            pltpu.VMEM((DEPTH, L2 * L2), f32),
            pltpu.VMEM((DEPTH, WINDOW), jnp.int32),
            pltpu.VMEM((1, DEPTH), jnp.int32),
            pltpu.SemaphoreType.DMA((3,)),
        ],
        compiler_params=pltpu.CompilerParams(vmem_limit_bytes=4 * MIB),
        name="packed_own",
    )(in_hbm(flat), in_hbm(members), in_hbm(species))


def split_kernel(piece, structure_hbm, parts_ref, buffer, sems):
    step_rows = PIECE_ROWS // SPLIT_STEPS

    def fetch(step):
        rows = pl.ds(piece * PIECE_ROWS + step * step_rows, step_rows)
        return pltpu.make_async_copy(structure_hbm.at[rows, :], buffer.at[step], sems.at[step])

    for step in range(SPLIT_STEPS):
        fetch(step).start()
    half = L2 // 2
    for step in range(SPLIT_STEPS):
        fetch(step).wait()

        def half_cell(i, carry, step=step):
            source = pl.ds(pl.multiple_of(i * half, half), half)
            target = step * 2 * step_rows + i // 2 * 2 * L2 + i % 2 * half
            high, low = halves(buffer[step, source, :])
            parts_ref[pl.ds(pl.multiple_of(target, half), half), :] = high
            parts_ref[pl.ds(pl.multiple_of(target + L2, half), half), :] = low
            return carry

        lax.fori_loop(0, step_rows // half, half_cell, 0, unroll=2)


def split_piece(piece, structure):
    return pl.pallas_call(
        functools.partial(split_kernel, piece),
        out_shape=jax.ShapeDtypeStruct((2 * PIECE_ROWS, ROWS), bf16),
        in_specs=[pl.BlockSpec(memory_space=pltpu.HBM)],
        out_specs=in_vmem(1)[0],
        scratch_shapes=[
            pltpu.VMEM((SPLIT_STEPS, PIECE_ROWS // SPLIT_STEPS, ROWS), f32),
            pltpu.SemaphoreType.DMA((SPLIT_STEPS,)),
        ],
        compiler_params=pltpu.CompilerParams(vmem_limit_bytes=12 * MIB),
        cost_estimate=pl.CostEstimate(
            flops=MIB, bytes_accessed=4 * PIECE_ROWS * ROWS, transcendentals=0
        ),
        name="split_piece",
    )(in_hbm(structure))


def both_tiles(own, below, above):
    lane = lane_index(own.shape)
    return [own, jnp.where(lane < 2 * L2, above, below)]


def setup_kernel(own_ref, below_ref, above_ref, table_hbm, member_ref, delta_ref, tile_ref, *rest):
    table_ref, table_tile, sem = rest
    copy = pltpu.make_async_copy(table_hbm, table_ref, sem.at[0])
    copy.start()
    cells = lax.broadcasted_iota(jnp.int32, (WINDOW, LANES), 0).astype(f32)
    group = lane_index((WINDOW, LANES)) // L2
    sources = [[own_ref] * DEPTH, [above_ref, above_ref, below_ref, below_ref]]
    for half, refs in enumerate(sources):
        member = jnp.zeros((WINDOW, LANES), f32)
        for g, ref in enumerate(refs):
            found = (ref[L2 + g : L2 + g + 1, :] == cells).astype(f32)
            found = jnp.max(found, axis=1, keepdims=True)
            member = jnp.where(group == g, found, member)
        member_ref[:, half * LANES : (half + 1) * LANES] = member
    tiles = both_tiles(own_ref[:L2, :], below_ref[:L2, :], above_ref[:L2, :])
    for half, tile in enumerate(tiles):
        tile_ref[:, half * LANES : (half + 1) * LANES] = tile

    copy.wait()
    tile_kernel(table_ref, table_tile)
    table = table_tile[...]
    turns = [table] + [pltpu.roll(table, m * L2, 1) for m in range(1, SPECIES)]
    group = lane_index((L2, LANES)) // L2
    thin = lane_index((1, LANES))
    row = slice(L2 + DEPTH, L2 + DEPTH + 1)
    for half, refs in enumerate(sources):
        delta = jnp.zeros((L2, LANES), f32)
        for g, ref in enumerate(refs):
            kinds = jnp.max(jnp.where(thin == g, ref[row, :], -1.0), axis=1, keepdims=True)
            for kind in range(SPECIES):
                here = (group == g) & (kinds == kind)
                delta = jnp.where(here, turns[(g - kind) % SPECIES], delta)
        delta_ref[:, half * LANES : (half + 1) * LANES] = delta


def setup(own, below, above, table):
    return pl.pallas_call(
        setup_kernel,
        out_shape=(
            jax.ShapeDtypeStruct((WINDOW, 2 * LANES), f32),
            jax.ShapeDtypeStruct((L2, 2 * LANES), f32),
            jax.ShapeDtypeStruct((L2, 2 * LANES), f32),
        ),
        in_specs=in_vmem(3) + [pl.BlockSpec(memory_space=pltpu.HBM)],
        out_specs=tuple(in_vmem(3)),
        scratch_shapes=[
            pltpu.VMEM((SPECIES, L2 * L2), f32),
            pltpu.VMEM((L2, LANES), f32),
            pltpu.SemaphoreType.DMA((1,)),
        ],
        compiler_params=pltpu.CompilerParams(vmem_limit_bytes=4 * MIB),
        name="setup",
    )(own, below, above, in_hbm(table))


def three_products(product):
    parts = product.reshape(-1, 2, L2, 2 * LANES)
    high, low = parts[:, 0], parts[:, 1]
    return (high[..., :LANES] + high[..., LANES:]) + low[..., :LANES]


def first_image_kernel(*refs):
    parts, (tile_ref, image_ref) = refs[:PIECES], refs[PIECES:]
    lane_tile = CENTRE * L2 // LANES * LANES
    before = CENTRE * L2 - lane_tile
    for half in range(2):
        lanes = slice(half * LANES, (half + 1) * LANES)
        right = jnp.concatenate(halves(tile_ref[:, lanes]), axis=1)
        right = jnp.concatenate(
            [
                jnp.zeros((before, 2 * LANES), bf16),
                right,
                jnp.zeros((LANES - before - L2, 2 * LANES), bf16),
            ],
            axis=0,
        )
        for piece, ref in enumerate(parts):
            left = ref[:, lane_tile : lane_tile + LANES]
            product = jnp.dot(left, right, preferred_element_type=f32)
            image_ref[piece * PIECE : (piece + 1) * PIECE, :, lanes] = three_products(product)


def first_images(parts, tile):
    return pl.pallas_call(
        first_image_kernel,
        out_shape=jax.ShapeDtypeStruct((WINDOW, L2, 2 * LANES), f32),
        in_specs=in_vmem(PIECES + 1),
        out_specs=in_vmem(1)[0],
        compiler_params=pltpu.CompilerParams(vmem_limit_bytes=8 * MIB),
        name="first_images",
    )(*parts, tile)


def site_blocks(tile):
    lane = lane_index((L2, LANES))
    masks = [(lane // L2 == s).astype(f32).astype(bf16) for s in range(DEPTH)]
    return jnp.concatenate([tile * mask for mask in masks], axis=0)


def moved(window, cell, half, image):
    blocks = jnp.concatenate([site_blocks(part) for part in halves(image)], axis=1)
    left = window[cell * 2 * L2 : (cell + 1) * 2 * L2, half * LANES : (half + 1) * LANES]
    return three_products(jnp.dot(left, blocks, preferred_element_type=f32))[0]


HIGH_AT = (1, 2)
LOW_AT = (0, 3)


def keep(column, place, half, value):
    rows = slice(place * L2, (place + 1) * L2)
    for at, part in zip((HIGH_AT[half], LOW_AT[half]), halves(value)):
        column[rows, at * LANES : (at + 1) * LANES] = part


def lane_runs(early):
    per_tile = LANES // L2
    runs = []
    for start in range(0, WINDOW, per_tile):
        cells = range(start, min(start + per_tile, WINDOW))
        if (len(cells) == per_tile and all(c in early_cells() for c in cells)) != early:
            continue
        low, high = cells[0] * L2, (cells[-1] + 1) * L2
        if runs and runs[-1][1] == low:
            runs[-1][1] = high
        else:
            runs.append([low, high])
    return runs


def joined(pieces, axis):
    return pieces[0] if len(pieces) == 1 else jnp.concatenate(pieces, axis=axis)


def set_images(parts, cells, column, slot, runs=((0, ROWS),), start=None):
    def rows_of(base):
        return joined([ref[base : base + L2, low:high] for low, high in runs], 1)

    def lanes_of(first, last):
        return joined([column[low:high, first:last] for low, high in runs], 0)

    high, low = [], []
    for cell in cells:
        ref, base = parts[cell // PIECE], cell % PIECE * 2 * L2
        high.append(rows_of(base))
        low.append(rows_of(base + L2))
    high, low = jnp.concatenate(high, axis=0), jnp.concatenate(low, axis=0)
    own = jnp.dot(high, lanes_of(0, 2 * LANES), preferred_element_type=f32)
    other = jnp.dot(high, lanes_of(2 * LANES, 4 * LANES), preferred_element_type=f32)
    both = jnp.dot(low, lanes_of(LANES, 3 * LANES), preferred_element_type=f32)
    shape = (len(cells), L2, LANES)
    own = own[:, :LANES] + own[:, LANES:] + both[:, :LANES]
    other = other[:, :LANES] + other[:, LANES:] + both[:, LANES:]
    for at, image in enumerate((own, other)):
        image = image.reshape(shape)
        lanes = slice(at * LANES, (at + 1) * LANES)
        if start is not None:
            image = image + start[cells[0] : cells[-1] + 1, :, lanes]
        slot[: len(cells), :, lanes] = image


def window_tiles(near, cell):
    dx, dy, dz = cell // 15, cell // 5 % 3, cell % 5 - 2
    own, below, above = (near(dx, dy, i) for i in range(3))
    group = lane_index((L2, LANES)) // L2
    first, second = own, jnp.where(group < 2, above, below)
    if dz > 0:
        first = jnp.where(group < dz, above, own)
        second = jnp.where(group < dz, own, jnp.where(group < 2 + dz, above, below))
    elif dz < 0:
        first = jnp.where(group >= DEPTH + dz, below, own)
        second = jnp.where(group >= DEPTH + dz, own, jnp.where(group < 2 + dz, above, below))
    move = -dz % DEPTH * L2
    return [tile if move == 0 else pltpu.roll(tile, move, 1) for tile in (first, second)]


def set_window(window, near, member_ref, cell):
    base = cell * 2 * L2
    for half, tile in enumerate(window_tiles(near, cell)):
        lanes = slice(half * LANES, (half + 1) * LANES)
        high, low = halves(tile * member_ref[cell : cell + 1, lanes])
        window[base : base + L2, lanes] = high
        window[base + L2 : base + 2 * L2, lanes] = low


def set_column(column, window, tile_ref, cell, image):
    for half in range(2):
        lanes = slice(half * LANES, (half + 1) * LANES)
        value = moved(window, cell, half, image[:, lanes])
        if cell == CENTRE:
            value = value + tile_ref[:, lanes]
        keep(column, cell, half, value)


def early_cells():
    return [cell for cell in range(WINDOW) if cell // 15 == 1 or cell // 5 % 3 == 1]


def near_slabs(own_ref, middle_refs, side_refs):
    def near(dx, dy, slab):
        if dx == 1:
            return own_ref[slab] if dy == 1 else middle_refs[dy // 2][slab]
        ref = side_refs[dy]
        return ref[dx // 2 % ref.shape[0], slab]

    return near


def sweep_chunks():
    return [list(range(base, min(base + CHUNK, WINDOW))) for base in range(0, WINDOW, CHUNK)]


def early_kernel(parts_count, *refs):
    parts, refs = refs[:parts_count], refs[parts_count:]
    own_ref, south_ref, north_ref, side_ref, member_ref, tile_ref, image_ref = refs[:7]
    column, window, start = refs[7:]
    near = near_slabs(own_ref, (south_ref, north_ref), (None, side_ref, None))
    for cell in early_cells():
        set_window(window, near, member_ref, cell)
    for cell in early_cells():
        set_column(column, window, tile_ref, cell, image_ref[cell])
    for cells in sweep_chunks():
        part = start.at[cells[0] : cells[-1] + 1]
        set_images(parts, cells, column, part, lane_runs(True))


def early_columns(parts, *operands):
    operands = (*parts, *operands)
    return pl.pallas_call(
        functools.partial(early_kernel, len(parts)),
        out_shape=(
            jax.ShapeDtypeStruct((ROWS, 4 * LANES), bf16),
            jax.ShapeDtypeStruct((2 * ROWS, 2 * LANES), bf16),
            jax.ShapeDtypeStruct((WINDOW, L2, 2 * LANES), f32),
        ),
        in_specs=in_vmem(len(operands)),
        out_specs=tuple(in_vmem(3)),
        compiler_params=pltpu.CompilerParams(vmem_limit_bytes=8 * MIB),
        name="early_columns",
    )(*operands)


def sweep_over(parts, chunks, source, use_image, slots, **options):
    for i, chunk in enumerate(chunks):
        set_images(parts, chunk, source, slots[i % 2], **options)
        if i > 0:
            use_image(i - 1, slots[(i - 1) % 2])
    use_image(len(chunks) - 1, slots[(len(chunks) - 1) % 2])


def delta_blocks(tile):
    high, low = (site_blocks(part) for part in halves(tile))
    return jnp.concatenate(
        [
            jnp.concatenate([high, low], axis=1),
            jnp.concatenate([high, jnp.zeros_like(high)], axis=1),
        ],
        axis=0,
    )


def last_sweep(parts, column, window, tile_ref, delta_ref, stage, sent, local, tau_ref, slots, final):
    deltas = [delta_blocks(delta_ref[:, half * LANES : (half + 1) * LANES]) for half in range(2)]
    group_of = lane_index((L2, LANES)) // L2
    lines = [
        (i, place, cell_of(ox, oy, 0))
        for i, group in enumerate(stage)
        for place, (ox, oy) in enumerate(group)
    ]
    step = stage_lines(stage)
    chunks = [lines[i : i + step] for i in range(0, len(lines), step)]
    places = [(at, oz) for at in range(step) for oz in range(-2, 3)]

    def use_image(number, slot):
        chunk = chunks[number]
        values = []
        for half in range(2):
            lanes = slice(half * LANES, (half + 1) * LANES)
            work = final.at[number % 2, half]
            for row, (at, oz) in enumerate(places[: 5 * len(chunk)]):
                if half == 1 and oz == 0:
                    continue
                cell = chunk[at][2] + oz
                value = moved(window, cell, half, slot[row, :, lanes])
                if cell == CENTRE:
                    value = value + tile_ref[:, lanes]
                    tau_ref[...] = value
                high, low = halves(value)
                work[row * L2 : (row + 1) * L2, :LANES] = high
                work[row * L2 : (row + 1) * L2, LANES:] = low
            count = 5 * len(chunk)
            product = jnp.dot(work[: count * L2, :], deltas[half], preferred_element_type=f32)
            product = product[:, :LANES] + product[:, LANES:]
            values.append(product.reshape(count, L2, LANES))
        for row, (at, oz) in enumerate(places[: 5 * len(chunk)]):
            i, place, _ = chunk[at]
            value = values[0][row]
            local[i][place * 5 + oz + 2] = value
            if oz > 0:
                value = jnp.where(group_of >= DEPTH - oz, values[1][row], value)
            elif oz < 0:
                value = jnp.where(group_of < -oz, values[1][row], value)
            if oz != 0:
                value = pltpu.roll(value, oz % DEPTH * L2, 1)
            sent[i][place * 5 + oz + 2] = value

    cells = [[middle + oz for _, _, middle in chunk for oz in range(-2, 3)] for chunk in chunks]
    sweep_over(parts, cells, column, use_image, slots)


def stage_lines(stage):
    return 2 if sum(len(group) for group in stage) > 2 else 1


def first_kernel(stage, *refs):
    parts, refs = refs[:PIECES], refs[PIECES:]
    early_column, early_window, start, image_ref, south_ref, north_ref = refs[:6]
    member_ref, tile_ref, delta_ref = refs[6:9]
    sent, local = refs[9 : 9 + len(stage)], refs[9 + len(stage) : 9 + 2 * len(stage)]
    column, window, other, slot_a, slot_b, final = refs[9 + 2 * len(stage) :]
    slots = (slot_a, slot_b)

    near = near_slabs(None, None, (south_ref, None, north_ref))
    for cell in early_cells():
        rows = slice(cell * L2, (cell + 1) * L2)
        column[rows, :] = early_column[rows, :]
        rows = slice(cell * 2 * L2, (cell + 1) * 2 * L2)
        window[rows, :] = early_window[rows, :]
    late = [cell for cell in range(WINDOW) if cell not in early_cells()]
    for cell in late:
        set_window(window, near, member_ref, cell)
    for cell in late:
        set_column(column, window, tile_ref, cell, image_ref[cell])
    source, target = column, other
    full = sweep_chunks()
    for sweep in range(1, ITERS - 1):

        def use_image(i, slot, target=target):
            for place, cell in enumerate(full[i]):
                set_column(target, window, tile_ref, cell, slot[place])

        if sweep == 1:
            options = dict(runs=lane_runs(False), start=start)
        else:
            options = {}
        sweep_over(parts, full, source, use_image, slots, **options)
        source, target = target, source
    if source is not column:
        column[...] = source[...]
    last_sweep(
        parts, column, window, tile_ref, delta_ref, stage, sent, local, None, slots, final
    )


def next_kernel(stage, *refs):
    parts, refs = refs[:PIECES], refs[PIECES:]
    column, window, tile_ref, delta_ref = refs[:4]
    sent, local = refs[4 : 4 + len(stage)], refs[4 + len(stage) : 4 + 2 * len(stage)]
    rest = refs[4 + 2 * len(stage) :]
    tau_ref = rest[0] if len(rest) == 4 else None
    slot_a, slot_b, final = rest[-3:]
    last_sweep(
        parts,
        column,
        window,
        tile_ref,
        delta_ref,
        stage,
        sent,
        local,
        tau_ref,
        (slot_a, slot_b),
        final,
    )


def stage_call(kernel, stage, extra_outs, extra_scratch, operands, flops):
    lines = stage_lines(stage)
    longest = max(CHUNK, 5 * lines)
    out_shape = [jax.ShapeDtypeStruct((5 * len(group), L2, LANES), f32) for group in stage] * 2
    out_shape += extra_outs
    return pl.pallas_call(
        functools.partial(kernel, stage),
        out_shape=tuple(out_shape),
        in_specs=in_vmem(len(operands)),
        out_specs=tuple(in_vmem(len(out_shape))),
        scratch_shapes=extra_scratch
        + [pltpu.VMEM((longest, L2, 2 * LANES), f32)] * 2
        + [pltpu.VMEM((2, 2, 5 * lines * L2, 2 * LANES), bf16)],
        compiler_params=pltpu.CompilerParams(vmem_limit_bytes=24 * MIB),
        cost_estimate=pl.CostEstimate(flops=flops, bytes_accessed=MIB, transcendentals=0),
    )(*operands)


def first_stage(stage, parts, *operands):
    return stage_call(
        first_kernel,
        stage,
        [
            jax.ShapeDtypeStruct((ROWS, 4 * LANES), bf16),
            jax.ShapeDtypeStruct((2 * ROWS, 2 * LANES), bf16),
        ],
        [pltpu.VMEM((ROWS, 4 * LANES), bf16)],
        (*parts, *operands),
        2 * 6 * (ITERS - 2) * ROWS * ROWS * LANES,
    )


def next_stage(stage, parts, column, window, tile, delta):
    tau = [jax.ShapeDtypeStruct((L2, LANES), f32)]
    return stage_call(
        next_kernel,
        stage,
        tau if any((0, 0) in group for group in stage) else [],
        [],
        (*parts, column, window, tile, delta),
        2 * ROWS * ROWS * LANES,
    )


def find_tile(groups, refs, ox, oy, oz):
    for group, ref in zip(groups, refs):
        if (ox, oy) in group:
            return ref[group.index((ox, oy)) * 5 + oz + 2]
    raise ValueError("no tile")


def plane_offsets():
    return [(ox, oy) for ox in (-1, 0, 1) for oy in (-1, 0, 1)]


def cell_of(dx, dy, dz):
    return ((dx + 1) * 3 + dy + 1) * 5 + dz + 2


def turn_kernel(groups, *refs):
    own, out = refs[:-1], refs[-1]
    lane = lane_index((L2, LANES))

    def cell_tile(cell):
        cell = min(cell, WINDOW - 1)
        return find_tile(groups, own, cell // 15 - 1, cell // 5 % 3 - 1, cell % 5 - 2)

    for base in range(0, WINDOW, DEPTH):
        block = jnp.concatenate([cell_tile(base + k) for k in range(DEPTH)], axis=0)
        turned = block.T
        pieces = [turned[s * L2 : (s + 1) * L2] for s in range(DEPTH)]
        for k in range(min(DEPTH, WINDOW - base)):
            value = pieces[0] if k == 0 else pltpu.roll(pieces[0], (-k % DEPTH) * L2, 1)
            for s in range(1, DEPTH):
                move = (s - k) % DEPTH
                piece = pieces[s] if move == 0 else pltpu.roll(pieces[s], move * L2, 1)
                value = jnp.where(lane // L2 == s, piece, value)
            out[base + k] = value


def turned_tiles(groups, own):
    return pl.pallas_call(
        functools.partial(turn_kernel, groups),
        out_shape=jax.ShapeDtypeStruct((WINDOW, L2, LANES), f32),
        in_specs=in_vmem(len(own)),
        out_specs=in_vmem(1)[0],
        compiler_params=pltpu.CompilerParams(vmem_limit_bytes=8 * MIB),
        cost_estimate=pl.CostEstimate(flops=MIB, bytes_accessed=2 * MIB, transcendentals=0),
        name="turned_tiles",
    )(*own)


def add_rows(groups, got, turned_ref, sums):
    for group, ref in zip(groups, got):
        for place, (ox, oy) in enumerate(group):
            for oz in range(-2, 3):
                cell = cell_of(-ox, -oy, -oz)
                value = ref[place * 5 + oz + 2] * turned_ref[cell]
                sums[cell : cell + 1, :] = jnp.sum(value, axis=0, keepdims=True)


def near_kernel(groups, *refs):
    got = refs[: len(groups)]
    turned_ref, tau_ref, sums, flat_ref = refs[len(groups) :]
    flat_kernel(tau_ref, flat_ref)
    sums[...] = jnp.zeros_like(sums)
    add_rows(groups, got, turned_ref, sums)


def near_sums(groups, got, turned, tau):
    return pl.pallas_call(
        functools.partial(near_kernel, groups),
        out_shape=(
            jax.ShapeDtypeStruct((SUM_ROWS, LANES), f32),
            jax.ShapeDtypeStruct((DEPTH, L2 * L2), f32),
        ),
        in_specs=in_vmem(len(got) + 2),
        out_specs=tuple(in_vmem(2)),
        compiler_params=pltpu.CompilerParams(vmem_limit_bytes=8 * MIB),
        name="near_sums",
    )(*got, turned, tau)


def total_kernel(groups, *refs):
    got = refs[: len(groups)]
    turned_ref, near_ref, out_ref, rows = refs[len(groups) :]
    rows[...] = near_ref[...]
    add_rows(groups, got, turned_ref, rows)
    sums = rows[...]
    site = lax.broadcasted_iota(jnp.int32, (8, LANES), 0)
    pick = (lane_index((8, LANES)) // L2 == site).astype(f32).astype(bf16)
    high = sums.astype(bf16)
    rest = sums - high.astype(f32)
    middle = rest.astype(bf16)
    low = (rest - middle.astype(f32)).astype(bf16)
    total = lax.dot_general(
        pick,
        jnp.concatenate([high, middle, low], axis=0),
        (((1,), (1,)), ((), ())),
        preferred_element_type=f32,
    )
    total = (total[:, :SUM_ROWS] + total[:, SUM_ROWS : 2 * SUM_ROWS]) + total[:, 2 * SUM_ROWS :]
    out_ref[...] = total[:DEPTH, :WINDOW]


def total_sums(groups, got, turned, near):
    return pl.pallas_call(
        functools.partial(total_kernel, groups),
        out_shape=jax.ShapeDtypeStruct((DEPTH, WINDOW), f32),
        in_specs=in_vmem(len(got) + 2),
        out_specs=in_vmem(1)[0],
        scratch_shapes=[pltpu.VMEM((SUM_ROWS, LANES), f32)],
        compiler_params=pltpu.CompilerParams(vmem_limit_bytes=8 * MIB),
        name="total_sums",
    )(*got, turned, near)


def plane_offsets():
    return [(ox, oy) for ox in (-1, 0, 1) for oy in (-1, 0, 1)]


def cell_of(dx, dy, dz):
    return ((dx + 1) * 3 + dy + 1) * 5 + dz + 2


def plane_groups():
    counts = (lax.axis_size("gx"), lax.axis_size("gy"))
    groups = {}
    for ox, oy in plane_offsets():
        groups.setdefault((ox % counts[0], oy % counts[1]), []).append((ox, oy))
    return groups


def body(t_matrix, structure, species, members, delta_table):
    own = packed_own(
        t_matrix.reshape(DEPTH, L2 * L2),
        members.reshape(DEPTH, WINDOW),
        species.reshape(1, DEPTH),
    )
    structure = structure[0]

    below, above = shifted(own, (0, 0, 1)), shifted(own, (0, 0, -1))
    parts = split_piece(0, structure)
    slabs = jnp.stack([own[:L2], below[:L2], above[:L2]])
    slabs, parts = lax.optimization_barrier((slabs, parts))
    parts = (parts,)
    sides = shifted(slabs, (1, 0, 0))[None]
    if lax.axis_size("gx") > 2:
        sides = jnp.stack([sides[0], shifted(slabs, (-1, 0, 0))])
    south, north = shifted(slabs, (0, 1, 0)), shifted(slabs, (0, -1, 0))
    prepared = setup(own, below, above, delta_table)
    sides, *prepared = lax.optimization_barrier((sides, *prepared))
    member, delta, tile = prepared
    side_south, side_north = shifted(sides, (0, 1, 0)), shifted(sides, (0, -1, 0))
    images = first_images(parts, tile)
    early = early_columns(parts, slabs, south, north, sides, member, tile, images)

    table = plane_groups()
    stages = [
        [shift for shift in table if shift[0] != 0 and shift[1] == 0],
        [shift for shift in table if shift[0] != 0 and shift[1] == 1],
        [shift for shift in table if shift[0] == 0 and shift[1] != 0],
        [shift for shift in table if shift[0] != 0 and shift[1] > 1],
        [(0, 0)],
    ]
    got, local = {}, {}
    for number, stage in enumerate(stages):
        groups = [table[shift] for shift in stage]
        if number == 0:
            *tiles, column, window = first_stage(
                groups, parts, *early, images, side_south, side_north, member, tile, delta
            )
        else:
            tiles = next_stage(groups, parts, column, window, tile, delta)
        if (0, 0) in stage:
            tau = tiles[-1]
        local.update(zip(stage, tiles[len(stage) :]))
        for shift, block in zip(stage, tiles):
            got[shift] = block if shift == (0, 0) else shifted(block, shift + (0,))
    shifts = list(table)
    turned = turned_tiles([table[shift] for shift in shifts], [local[shift] for shift in shifts])
    near_rows, site_tau = near_sums([table[0, 0]], [got[0, 0]], turned, tau)
    far = [shift for shift in shifts if shift != (0, 0)]
    pairs = total_sums(
        [table[shift] for shift in far], [got[shift] for shift in far], turned, near_rows
    )
    return (
        site_tau.reshape(1, 1, 1, DEPTH, L2 * L2),
        pairs.reshape(1, 1, DEPTH, WINDOW),
    )


def solution(mesh):
    placed = (
        P(None, "gx", "gy", "gz", None),
        P(),
        P("gx", "gy", "gz"),
        P("gx", "gy", "gz", None),
        P(),
    )
    return jax.shard_map(
        body,
        mesh=mesh,
        in_specs=placed,
        out_specs=(P(None, "gx", "gy", "gz", None), P("gx", "gy", "gz", None)),
        check_vma=False,
    )
```

profile of v0, /device:TPU:0, one launch (start us, length us, event | category | flops | bytes accessed | tf_op | source)
XLA Modules:
  0.0 47.6 jit_solution(563072723563499041)
XLA Ops:
  0.6 0.9 %packed_own.1.own_ref = f32[40,128]{1,0:T(8,128)S(1)} custom-call(f32[4,1024]{1,0:T(4,128)} %bitcast.17, s32[4,45]{1,0:T(4,128)} %bitcast.19, s32[1,4]{1,0:T(1,128)} %bitcast.20), custom_call_target="tpu_custom_call" | custom-call | tf_op jit(solution)/shard_map/packed_own/pallas_call | solution.py:112
  1.5 5.1 %collective-permute-start.1 = (f32[40,128]{1,0:T(8,128)S(1)}, f32[40,128]{1,0:T(8,128)S(1)}, u32[]{:S(2)}, u32[]{:S(2)}) collective-permute-start(f32[40,128]{1,0:T(8,128)S(1)} %packed_own.1.own_ref), channel_id=1, source_target_pairs={{0,3},{1,0},{2,1},{3,2},{4,7},{5,4},{6,5},{7,6},{8,11},{9,8},{10,9... | collective-permute-start | bytes 61448 | tf_op jit(solution)/shard_map/ppermute | solution.py:43
  6.6 0.0 collective-permute-start
  6.6 3.8 %split_piece.1.refs_0_ = bf16[2880,1440]{1,0:T(8,128)(2,1)S(1)} custom-call(f32[1440,1440]{1,0:T(8,128)} %bitcast.16), custom_call_target="tpu_custom_call" | custom-call | flops 1048576 | bytes 8294400 | tf_op jit(solution)/shard_map/split_piece/pallas_call | solution.py:153
  10.4 0.0 collective-permute-done.1.above_ref
  10.5 1.8 %collective-permute-done.below_ref = f32[40,128]{1,0:T(8,128)S(1)} collective-permute-done((f32[40,128]{1,0:T(8,128)S(1)}, f32[40,128]{1,0:T(8,128)S(1)}, u32[]{:S(2)}, u32[]{:S(2)}) %collective-permute-start) | collective-permute-done | bytes 20512 | tf_op jit(solution)/shard_map/ppermute | solution.py:43
  12.2 1.5 %collective-permute-start.4 = (f32[3,32,128]{2,1,0:T(8,128)S(1)}, f32[3,32,128]{2,1,0:T(8,128)S(1)}, u32[]{:S(2)}, u32[]{:S(2)}) collective-permute-start(f32[3,32,128]{2,1,0:T(8,128)S(1)} %pad_maximum_fusion.refs_1_), channel_id=1, source_target_pairs={{0,16},{1,17},{2,18},{3,19},{4,20},{5,21},{6,22},{7,23},{8,24},{9,... | collective-permute-start | bytes 147464 | tf_op jit(solution)/shard_map/ppermute | solution.py:43
  13.8 0.0 collective-permute-start.3
  13.8 0.5 %collective-permute-start.2 = (f32[3,32,128]{2,1,0:T(8,128)S(1)}, f32[3,32,128]{2,1,0:T(8,128)S(1)}, u32[]{:S(2)}, u32[]{:S(2)}) collective-permute-start(f32[3,32,128]{2,1,0:T(8,128)S(1)} %pad_maximum_fusion.refs_1_), channel_id=1, source_target_pairs={{0,4},{1,5},{2,6},{3,7},{4,8},{5,9},{6,10},{7,11},{8,12},{9,13},{1... | collective-permute-start | bytes 147464 | tf_op jit(solution)/shard_map/ppermute | solution.py:43
  14.3 0.9 %setup.1 = (f32[45,256]{1,0:T(8,128)S(1)}, f32[32,256]{1,0:T(8,128)S(1)}, f32[32,256]{1,0:T(8,128)S(1)}) custom-call(f32[40,128]{1,0:T(8,128)S(1)} %packed_own.1.own_ref, f32[40,128]{1,0:T(8,128)S(1)} %collective-permute-done.below_ref, f32[40,128]{1,0:T(8,128)S(1)} %collective-permute-done.1.above_ref, f32[4,1024]{1,0:T(4,128)} %table_hbm.1), custom_call_target="tpu_custom_call" | custom-call | tf_op jit(solution)/shard_map/setup/pallas_call | solution.py:211
  15.2 1.1 %collective-permute-done.4 = f32[3,32,128]{2,1,0:T(8,128)S(1)} collective-permute-done((f32[3,32,128]{2,1,0:T(8,128)S(1)}, f32[3,32,128]{2,1,0:T(8,128)S(1)}, u32[]{:S(2)}, u32[]{:S(2)}) %collective-permute-start.4) | collective-permute-done | bytes 49184 | tf_op jit(solution)/shard_map/ppermute | solution.py:43
  16.4 0.2 collective-permute-start.6
  16.5 0.3 collective-permute-start.5
  16.9 0.9 %first_images.1.refs_7_.refs_4_ = f32[45,32,256]{2,1,0:T(8,128)S(1)} custom-call(bf16[2880,1440]{1,0:T(8,128)(2,1)S(1)} %split_piece.1.refs_0_, f32[32,256]{1,0:T(8,128)S(1)} %get-tuple-element.38.refs_1_.refs_6_.refs_8_.refs_3_), custom_call_target="tpu_custom_call" | custom-call | tf_op jit(solution)/shard_map/first_images/pallas_call | solution.py:258
  17.8 0.0 collective-permute-done.3.refs_3_
  17.8 0.0 collective-permute-done.2.refs_2_
  17.8 2.0 %early_columns.1 = (bf16[1440,512]{1,0:T(8,128)(2,1)S(1)}, bf16[2880,256]{1,0:T(8,128)(2,1)S(1)}, f32[45,32,256]{2,1,0:T(8,128)S(1)}) custom-call(bf16[2880,1440]{1,0:T(8,128)(2,1)S(1)} %split_piece.1.refs_0_, f32[3,32,128]{2,1,0:T(8,128)S(1)} %pad_maximum_fusion.refs_1_, f32[3,32,128]{2,1,0:T(8,128)S(1)} %collective-permute-done.2.refs_2_, ...), custom_call_target="tpu_custom_call" | custom-call | tf_op jit(solution)/shard_map/early_columns/pallas_call | solution.py:403
  19.8 0.0 collective-permute-done.6.refs_6_
  19.8 0.7 %collective-permute-done.5.refs_5_ = f32[1,3,32,128]{3,2,1,0:T(8,128)S(1)} collective-permute-done((f32[1,3,32,128]{3,2,1,0:T(8,128)S(1)}, f32[1,3,32,128]{3,2,1,0:T(8,128)S(1)}, u32[]{:S(2)}, u32[]{:S(2)}) %collective-permute-start.5) | collective-permute-done | bytes 49184 | tf_op jit(solution)/shard_map/ppermute | solution.py:43
  20.5 9.4 %shard_map.68 = (f32[10,32,128]{2,1,0:T(8,128)S(1)}, f32[10,32,128]{2,1,0:T(8,128)S(1)}, bf16[1440,512]{1,0:T(8,128)(2,1)S(1)}, bf16[2880,256]{1,0:T(8,128)(2,1)S(1)}) custom-call(bf16[2880,1440]{1,0:T(8,128)(2,1)S(1)} %split_piece.1.refs_0_, bf16[1440,512]{1,0:T(8,128)(2,1)S(1)} %get-tuple-element.39.refs_1_, ...), custom_call_target="tpu_custom_call" | custom-call | flops 6370099200 | bytes 1048576 | tf_op jit(solution)/shard_map/pallas_call | solution.py:556
  29.9 1.6 %shard_map.71 = (f32[10,32,128]{2,1,0:T(8,128)S(1)}, f32[10,32,128]{2,1,0:T(8,128)S(1)}) custom-call(bf16[2880,1440]{1,0:T(8,128)(2,1)S(1)} %split_piece.1.refs_0_, bf16[1440,512]{1,0:T(8,128)(2,1)S(1)} %get-tuple-element.43.refs_1_, bf16[2880,256]{1,0:T(8,128)(2,1)S(1)} %get-tuple-element.44.refs_2_, ...), custom_call_target="tpu_custom_call" | custom-call | flops 530841600 | bytes 1048576 | tf_op jit(solution)/shard_map/pallas_call | solution.py:556
  31.5 1.7 %shard_map.70 = (f32[10,32,128]{2,1,0:T(8,128)S(1)}, f32[10,32,128]{2,1,0:T(8,128)S(1)}) custom-call(bf16[2880,1440]{1,0:T(8,128)(2,1)S(1)} %split_piece.1.refs_0_, bf16[1440,512]{1,0:T(8,128)(2,1)S(1)} %get-tuple-element.43.refs_1_, bf16[2880,256]{1,0:T(8,128)(2,1)S(1)} %get-tuple-element.44.refs_2_, ...), custom_call_target="tpu_custom_call" | custom-call | flops 530841600 | bytes 1048576 | tf_op jit(solution)/shard_map/pallas_call | solution.py:556
  33.2 1.4 %collective-permute-start.8 = (f32[10,32,128]{2,1,0:T(8,128)S(1)}, f32[10,32,128]{2,1,0:T(8,128)S(1)}, u32[]{:S(2)}, u32[]{:S(2)}) collective-permute-start(f32[10,32,128]{2,1,0:T(8,128)S(1)} %get-tuple-element.55), channel_id=1, source_target_pairs={{0,16},{1,17},{2,18},{3,19},{4,20},{5,21},{6,22},{7,23},{8,24},{9,... | collective-permute-start | bytes 491528 | tf_op jit(solution)/shard_map/ppermute | solution.py:43
  34.6 0.6 %collective-permute-start.9 = (f32[10,32,128]{2,1,0:T(8,128)S(1)}, f32[10,32,128]{2,1,0:T(8,128)S(1)}, u32[]{:S(2)}, u32[]{:S(2)}) collective-permute-start(f32[10,32,128]{2,1,0:T(8,128)S(1)} %get-tuple-element.56), channel_id=1, source_target_pairs={{0,20},{1,21},{2,22},{3,23},{4,24},{5,25},{6,26},{7,27},{8,28},{9,... | collective-permute-start | bytes 491528 | tf_op jit(solution)/shard_map/ppermute | solution.py:43
  35.3 2.0 %collective-permute-start.7 = (f32[10,32,128]{2,1,0:T(8,128)S(1)}, f32[10,32,128]{2,1,0:T(8,128)S(1)}, u32[]{:S(2)}, u32[]{:S(2)}) collective-permute-start(f32[10,32,128]{2,1,0:T(8,128)S(1)} %get-tuple-element.54), channel_id=1, source_target_pairs={{0,28},{1,29},{2,30},{3,31},{4,16},{5,17},{6,18},{7,19},{8,20},{9,... | collective-permute-start | bytes 491528 | tf_op jit(solution)/shard_map/ppermute | solution.py:43
  37.3 1.6 %shard_map.72 = (f32[5,32,128]{2,1,0:T(8,128)S(1)}, f32[5,32,128]{2,1,0:T(8,128)S(1)}, f32[5,32,128]{2,1,0:T(8,128)S(1)}, f32[5,32,128]{2,1,0:T(8,128)S(1)}) custom-call(bf16[2880,1440]{1,0:T(8,128)(2,1)S(1)} %split_piece.1.refs_0_, bf16[1440,512]{1,0:T(8,128)(2,1)S(1)} %get-tuple-element.43.refs_1_, bf16[2880,256]{1,0:T(8,128)(2,1)S(1)} %get-tuple-element.44.refs_2_, ...), custom_call_target="tpu_custom_call" | custom-call | flops 530841600 | bytes 1048576 | tf_op jit(solution)/shard_map/pallas_call | solution.py:556
  38.8 0.0 collective-permute-start.10
  38.9 0.5 %collective-permute-start.11 = (f32[5,32,128]{2,1,0:T(8,128)S(1)}, f32[5,32,128]{2,1,0:T(8,128)S(1)}, u32[]{:S(2)}, u32[]{:S(2)}) collective-permute-start(f32[5,32,128]{2,1,0:T(8,128)S(1)} %get-tuple-element.58), channel_id=1, source_target_pairs={{0,4},{1,5},{2,6},{3,7},{4,8},{5,9},{6,10},{7,11},{8,12},{9,13},{1... | collective-permute-start | bytes 245768 | tf_op jit(solution)/shard_map/ppermute | solution.py:43
  39.4 1.2 %shard_map.69 = (f32[5,32,128]{2,1,0:T(8,128)S(1)}, f32[5,32,128]{2,1,0:T(8,128)S(1)}, f32[32,128]{1,0:T(8,128)S(1)}) custom-call(bf16[2880,1440]{1,0:T(8,128)(2,1)S(1)} %split_piece.1.refs_0_, bf16[1440,512]{1,0:T(8,128)(2,1)S(1)} %get-tuple-element.43.refs_1_, bf16[2880,256]{1,0:T(8,128)(2,1)S(1)} %get-tuple-element.44.refs_2_, ...), custom_call_target="tpu_custom_call" | custom-call | flops 530841600 | bytes 1048576 | tf_op jit(solution)/shard_map/pallas_call | solution.py:556
  40.6 0.9 %turned_tiles.1.refs_1_.refs_5_ = f32[45,32,128]{2,1,0:T(8,128)S(1)} custom-call(f32[10,32,128]{2,1,0:T(8,128)S(1)} %get-tuple-element.46.refs_0_, f32[10,32,128]{2,1,0:T(8,128)S(1)} %get-tuple-element.47.refs_1_, f32[10,32,128]{2,1,0:T(8,128)S(1)} %get-tuple-element.48.refs_2_, f32[5,32,128]{2,1,0:T(8,128)S(1)} %get-tuple-element.49.refs_3_, ...), custom_call_target="tpu_custom_call" | custom-call | flops 1048576 | bytes 2097152 | tf_op jit(solution)/shard_map/turned_tiles/pallas_call | solution.py:632
  41.5 0.7 %near_sums.1 = (f32[48,128]{1,0:T(8,128)S(1)}, f32[4,1024]{1,0:T(4,128)}) custom-call(f32[5,32,128]{2,1,0:T(8,128)S(1)} %get-tuple-element.45.refs_0_, f32[45,32,128]{2,1,0:T(8,128)S(1)} %turned_tiles.1.refs_1_.refs_5_, f32[32,128]{1,0:T(8,128)S(1)} %get-tuple-element.52.refs_2_), custom_call_target="tpu_custom_call" | custom-call | tf_op jit(solution)/shard_map/near_sums/pallas_call | solution.py:661
  42.2 0.2 collective-permute-done.10.refs_3_
  42.4 1.4 %collective-permute-done.11.refs_4_ = f32[5,32,128]{2,1,0:T(8,128)S(1)} collective-permute-done((f32[5,32,128]{2,1,0:T(8,128)S(1)}, f32[5,32,128]{2,1,0:T(8,128)S(1)}, u32[]{:S(2)}, u32[]{:S(2)}) %collective-permute-start.11) | collective-permute-done | bytes 81952 | tf_op jit(solution)/shard_map/ppermute | solution.py:43
  43.8 0.0 collective-permute-done.8.refs_1_
  43.8 0.0 collective-permute-done.9.refs_2_
  43.8 2.9 %collective-permute-done.7.refs_0_ = f32[10,32,128]{2,1,0:T(8,128)S(1)} collective-permute-done((f32[10,32,128]{2,1,0:T(8,128)S(1)}, f32[10,32,128]{2,1,0:T(8,128)S(1)}, u32[]{:S(2)}, u32[]{:S(2)}) %collective-permute-start.7) | collective-permute-done | bytes 163872 | tf_op jit(solution)/shard_map/ppermute | solution.py:43
  46.7 0.9 %total_sums.1 = f32[4,45]{1,0:T(4,128)} custom-call(f32[10,32,128]{2,1,0:T(8,128)S(1)} %collective-permute-done.7.refs_0_, f32[10,32,128]{2,1,0:T(8,128)S(1)} %collective-permute-done.8.refs_1_, f32[10,32,128]{2,1,0:T(8,128)S(1)} %collective-permute-done.9.refs_2_, f32[5,32,128]{2,1,0:T(8,128)S(1)} %collective-permute-done.10.refs_3_, ...), custom_call_target="tpu_custom_call" | custom-call | tf_op jit(solution)/shard_map/total_sums/pallas_call | solution.py:697
  (4 shorter events, 0.0 us)
Async XLA Ops:
  1.5 8.9 %collective-permute-start.1 = (f32[40,128]{1,0:T(8,128)S(1)}, f32[40,128]{1,0:T(8,128)S(1)}, u32[]{:S(2)}, u32[]{:S(2)}) collective-permute-start(f32[40,128]{1,0:T(8,128)S(1)} %packed_own.1.own_ref), channel_id=1, source_target_pairs={{0,3},{1,0},{2,1},{3,2},{4,7},{5,4},{6,5},{7,6},{8,11},{9,8},{10,9... | collective-permute-start | bytes 61448 | tf_op jit(solution)/shard_map/ppermute | solution.py:43
  6.6 5.6 %collective-permute-start = (f32[40,128]{1,0:T(8,128)S(1)}, f32[40,128]{1,0:T(8,128)S(1)}, u32[]{:S(2)}, u32[]{:S(2)}) collective-permute-start(f32[40,128]{1,0:T(8,128)S(1)} %packed_own.1.own_ref), channel_id=1, source_target_pairs={{0,1},{1,2},{2,3},{3,0},{4,5},{5,6},{6,7},{7,4},{8,9},{9,10},{10,1... | collective-permute-start | bytes 61448 | tf_op jit(solution)/shard_map/ppermute | solution.py:43
  12.2 4.1 %collective-permute-start.4 = (f32[3,32,128]{2,1,0:T(8,128)S(1)}, f32[3,32,128]{2,1,0:T(8,128)S(1)}, u32[]{:S(2)}, u32[]{:S(2)}) collective-permute-start(f32[3,32,128]{2,1,0:T(8,128)S(1)} %pad_maximum_fusion.refs_1_), channel_id=1, source_target_pairs={{0,16},{1,17},{2,18},{3,19},{4,20},{5,21},{6,22},{7,23},{8,24},{9,... | collective-permute-start | bytes 147464 | tf_op jit(solution)/shard_map/ppermute | solution.py:43
  13.8 4.0 %collective-permute-start.3 = (f32[3,32,128]{2,1,0:T(8,128)S(1)}, f32[3,32,128]{2,1,0:T(8,128)S(1)}, u32[]{:S(2)}, u32[]{:S(2)}) collective-permute-start(f32[3,32,128]{2,1,0:T(8,128)S(1)} %pad_maximum_fusion.refs_1_), channel_id=1, source_target_pairs={{0,12},{1,13},{2,14},{3,15},{4,0},{5,1},{6,2},{7,3},{8,4},{9,5},{1... | collective-permute-start | bytes 147464 | tf_op jit(solution)/shard_map/ppermute | solution.py:43
  13.8 4.0 %collective-permute-start.2 = (f32[3,32,128]{2,1,0:T(8,128)S(1)}, f32[3,32,128]{2,1,0:T(8,128)S(1)}, u32[]{:S(2)}, u32[]{:S(2)}) collective-permute-start(f32[3,32,128]{2,1,0:T(8,128)S(1)} %pad_maximum_fusion.refs_1_), channel_id=1, source_target_pairs={{0,4},{1,5},{2,6},{3,7},{4,8},{5,9},{6,10},{7,11},{8,12},{9,13},{1... | collective-permute-start | bytes 147464 | tf_op jit(solution)/shard_map/ppermute | solution.py:43
  16.4 3.4 %collective-permute-start.6 = (f32[1,3,32,128]{3,2,1,0:T(8,128)S(1)}, f32[1,3,32,128]{3,2,1,0:T(8,128)S(1)}, u32[]{:S(2)}, u32[]{:S(2)}) collective-permute-start(f32[1,3,32,128]{3,2,1,0:T(8,128)S(1)} %bitcast.13), channel_id=1, source_target_pairs={{0,12},{1,13},{2,14},{3,15},{4,0},{5,1},{6,2},{7,3},{8,4},{9,5},{1... | collective-permute-start | bytes 147464 | tf_op jit(solution)/shard_map/ppermute | solution.py:43
  16.5 4.0 %collective-permute-start.5 = (f32[1,3,32,128]{3,2,1,0:T(8,128)S(1)}, f32[1,3,32,128]{3,2,1,0:T(8,128)S(1)}, u32[]{:S(2)}, u32[]{:S(2)}) collective-permute-start(f32[1,3,32,128]{3,2,1,0:T(8,128)S(1)} %bitcast.14), channel_id=1, source_target_pairs={{0,4},{1,5},{2,6},{3,7},{4,8},{5,9},{6,10},{7,11},{8,12},{9,13},{1... | collective-permute-start | bytes 147464 | tf_op jit(solution)/shard_map/ppermute | solution.py:43
  33.2 10.5 %collective-permute-start.8 = (f32[10,32,128]{2,1,0:T(8,128)S(1)}, f32[10,32,128]{2,1,0:T(8,128)S(1)}, u32[]{:S(2)}, u32[]{:S(2)}) collective-permute-start(f32[10,32,128]{2,1,0:T(8,128)S(1)} %get-tuple-element.55), channel_id=1, source_target_pairs={{0,16},{1,17},{2,18},{3,19},{4,20},{5,21},{6,22},{7,23},{8,24},{9,... | collective-permute-start | bytes 491528 | tf_op jit(solution)/shard_map/ppermute | solution.py:43
  34.6 9.2 %collective-permute-start.9 = (f32[10,32,128]{2,1,0:T(8,128)S(1)}, f32[10,32,128]{2,1,0:T(8,128)S(1)}, u32[]{:S(2)}, u32[]{:S(2)}) collective-permute-start(f32[10,32,128]{2,1,0:T(8,128)S(1)} %get-tuple-element.56), channel_id=1, source_target_pairs={{0,20},{1,21},{2,22},{3,23},{4,24},{5,25},{6,26},{7,27},{8,28},{9,... | collective-permute-start | bytes 491528 | tf_op jit(solution)/shard_map/ppermute | solution.py:43
  35.3 11.4 %collective-permute-start.7 = (f32[10,32,128]{2,1,0:T(8,128)S(1)}, f32[10,32,128]{2,1,0:T(8,128)S(1)}, u32[]{:S(2)}, u32[]{:S(2)}) collective-permute-start(f32[10,32,128]{2,1,0:T(8,128)S(1)} %get-tuple-element.54), channel_id=1, source_target_pairs={{0,28},{1,29},{2,30},{3,31},{4,16},{5,17},{6,18},{7,19},{8,20},{9,... | collective-permute-start | bytes 491528 | tf_op jit(solution)/shard_map/ppermute | solution.py:43
  38.8 3.6 %collective-permute-start.10 = (f32[5,32,128]{2,1,0:T(8,128)S(1)}, f32[5,32,128]{2,1,0:T(8,128)S(1)}, u32[]{:S(2)}, u32[]{:S(2)}) collective-permute-start(f32[5,32,128]{2,1,0:T(8,128)S(1)} %get-tuple-element.57), channel_id=1, source_target_pairs={{0,12},{1,13},{2,14},{3,15},{4,0},{5,1},{6,2},{7,3},{8,4},{9,5},{1... | collective-permute-start | bytes 245768 | tf_op jit(solution)/shard_map/ppermute | solution.py:43
  38.9 4.9 %collective-permute-start.11 = (f32[5,32,128]{2,1,0:T(8,128)S(1)}, f32[5,32,128]{2,1,0:T(8,128)S(1)}, u32[]{:S(2)}, u32[]{:S(2)}) collective-permute-start(f32[5,32,128]{2,1,0:T(8,128)S(1)} %get-tuple-element.58), channel_id=1, source_target_pairs={{0,4},{1,5},{2,6},{3,7},{4,8},{5,9},{6,10},{7,11},{8,12},{9,13},{1... | collective-permute-start | bytes 245768 | tf_op jit(solution)/shard_map/ppermute | solution.py:43
where the time goes:
time: 48 us; the launch traced here: 47.6 us
  Pallas kernels  26.5 us (55%)
  starting transfers between devices  12.3 us (26%)
  waiting for transfers between devices  8.06 us (17%)
  between operations  0.74 us (2%)
    pallas_call x5, Pallas kernels, stage_call(): pl.pallas_call(functools.partial(kernel, stage), out_shape=tuple(out_shap...  15.5 us
    ppermute x12, starting transfers between devices, shifted(): return lax.ppermute(x, MESH_AXES, pairs)  12.3 us
    ppermute x12, waiting for transfers between devices, shifted(): return lax.ppermute(x, MESH_AXES, pairs)  8.06 us
    pallas_call x1, Pallas kernels, split_piece(): pl.pallas_call(functools.partial(split_kernel, piece), out_shape=jax.Shap...  3.78 us
    pallas_call x1, Pallas kernels, early_columns(): pl.pallas_call(functools.partial(early_kernel, len(parts)), out_shape=(ja...  1.99 us
  transfers between devices with their start and end apart: 12, of which 6 were waited for; matrix products, arithmetic and copies ran while one was open for 0% of the time, Pallas kernels for 25%

commit v1 on v0

--- a/solution.py
+++ b/solution.py
@@ -25,6 +25,8 @@
 SPLIT_STEPS = 9
 CHUNK = 23
 MESH_AXES = ("gx", "gy", "gz")
+
+PLAN = (("x",), ("xy+", "y+"), ("xy-", "y-"), ("own",))
 
 
 bf16 = jnp.bfloat16
@@ -713,6 +715,14 @@
     return ((dx + 1) * 3 + dy + 1) * 5 + dz + 2
 
 
+def kind_of(shift):
+    if shift == (0, 0):
+        return "own"
+    if shift[1] == 0:
+        return "x"
+    return ("y" if shift[0] == 0 else "xy") + ("+" if shift[1] == 1 else "-")
+
+
 def plane_groups():
     counts = (lax.axis_size("gx"), lax.axis_size("gy"))
     groups = {}
@@ -746,13 +756,7 @@
     early = early_columns(parts, slabs, south, north, sides, member, tile, images)
 
     table = plane_groups()
-    stages = [
-        [shift for shift in table if shift[0] != 0 and shift[1] == 0],
-        [shift for shift in table if shift[0] != 0 and shift[1] == 1],
-        [shift for shift in table if shift[0] == 0 and shift[1] != 0],
-        [shift for shift in table if shift[0] != 0 and shift[1] > 1],
-        [(0, 0)],
-    ]
+    stages = [[shift for shift in table if kind_of(shift) in kinds] for kinds in PLAN]
     got, local = {}, {}
     for number, stage in enumerate(stages):
         groups = [table[shift] for shift in stage]

time: 48 us -> 48.9 us (1.019)
  starting transfers between devices: 12.3 us -> 13.4 us
  Pallas kernels: 26.5 us -> 25.9 us
    ppermute x12, starting transfers between devices: 12.3 us -> 13.4 us  [shifted(): return lax.ppermute(x, MESH_AXES, pairs)]
    pallas_call x5 -> x4, Pallas kernels: 15.5 us -> 14.9 us  [stage_call(): pl.pallas_call(functools.partial(kernel, stage), out_shape=tuple(out_shap...]
  transfers between devices with their start and end apart: 12 -> 12, of which waited for: 6 -> 6; matrix products, arithmetic and copies ran while one was open for 0% -> 0% of each run, Pallas kernels for 25% -> 21%
where the time goes in v1:
time: 48.9 us; the launch traced here: 48.6 us
  Pallas kernels  25.9 us (53%)
  starting transfers between devices  13.4 us (27%)
  waiting for transfers between devices  8.46 us (17%)
  between operations  0.73 us (1%)
    pallas_call x4, Pallas kernels, stage_call(): pl.pallas_call(functools.partial(kernel, stage), out_shape=tuple(out_shap...  14.9 us
    ppermute x12, starting transfers between devices, shifted(): return lax.ppermute(x, MESH_AXES, pairs)  13.4 us
    ppermute x12, waiting for transfers between devices, shifted(): return lax.ppermute(x, MESH_AXES, pairs)  8.46 us
    pallas_call x1, Pallas kernels, split_piece(): pl.pallas_call(functools.partial(split_kernel, piece), out_shape=jax.Shap...  3.78 us
    pallas_call x1, Pallas kernels, early_columns(): pl.pallas_call(functools.partial(early_kernel, len(parts)), out_shape=(ja...  1.99 us
  transfers between devices with their start and end apart: 12, of which 6 were waited for; matrix products, arithmetic and copies ran while one was open for 0% of the time, Pallas kernels for 21%

profile of v1, /device:TPU:0, one launch (start us, length us, event | category | flops | bytes accessed | tf_op | source)
XLA Modules:
  0.0 48.6 jit_solution(792460541267239000)
XLA Ops:
  0.6 0.9 %packed_own.1.own_ref = f32[40,128]{1,0:T(8,128)S(1)} custom-call(f32[4,1024]{1,0:T(4,128)} %bitcast.17, s32[4,45]{1,0:T(4,128)} %bitcast.19, s32[1,4]{1,0:T(1,128)} %bitcast.20), custom_call_target="tpu_custom_call" | custom-call | tf_op jit(solution)/shard_map/packed_own/pallas_call | solution.py:114
  1.5 5.1 %collective-permute-start.1 = (f32[40,128]{1,0:T(8,128)S(1)}, f32[40,128]{1,0:T(8,128)S(1)}, u32[]{:S(2)}, u32[]{:S(2)}) collective-permute-start(f32[40,128]{1,0:T(8,128)S(1)} %packed_own.1.own_ref), channel_id=1, source_target_pairs={{0,3},{1,0},{2,1},{3,2},{4,7},{5,4},{6,5},{7,6},{8,11},{9,8},{10,9... | collective-permute-start | bytes 61448 | tf_op jit(solution)/shard_map/ppermute | solution.py:45
  6.6 0.0 collective-permute-start
  6.6 3.8 %split_piece.1.refs_0_ = bf16[2880,1440]{1,0:T(8,128)(2,1)S(1)} custom-call(f32[1440,1440]{1,0:T(8,128)} %bitcast.16), custom_call_target="tpu_custom_call" | custom-call | flops 1048576 | bytes 8294400 | tf_op jit(solution)/shard_map/split_piece/pallas_call | solution.py:155
  10.4 0.0 collective-permute-done.1.above_ref
  10.5 1.8 %collective-permute-done.below_ref = f32[40,128]{1,0:T(8,128)S(1)} collective-permute-done((f32[40,128]{1,0:T(8,128)S(1)}, f32[40,128]{1,0:T(8,128)S(1)}, u32[]{:S(2)}, u32[]{:S(2)}) %collective-permute-start) | collective-permute-done | bytes 20512 | tf_op jit(solution)/shard_map/ppermute | solution.py:45
  12.2 1.5 %collective-permute-start.4 = (f32[3,32,128]{2,1,0:T(8,128)S(1)}, f32[3,32,128]{2,1,0:T(8,128)S(1)}, u32[]{:S(2)}, u32[]{:S(2)}) collective-permute-start(f32[3,32,128]{2,1,0:T(8,128)S(1)} %pad_maximum_fusion.refs_1_), channel_id=1, source_target_pairs={{0,16},{1,17},{2,18},{3,19},{4,20},{5,21},{6,22},{7,23},{8,24},{9,... | collective-permute-start | bytes 147464 | tf_op jit(solution)/shard_map/ppermute | solution.py:45
  13.8 0.0 collective-permute-start.3
  13.8 0.5 %collective-permute-start.2 = (f32[3,32,128]{2,1,0:T(8,128)S(1)}, f32[3,32,128]{2,1,0:T(8,128)S(1)}, u32[]{:S(2)}, u32[]{:S(2)}) collective-permute-start(f32[3,32,128]{2,1,0:T(8,128)S(1)} %pad_maximum_fusion.refs_1_), channel_id=1, source_target_pairs={{0,4},{1,5},{2,6},{3,7},{4,8},{5,9},{6,10},{7,11},{8,12},{9,13},{1... | collective-permute-start | bytes 147464 | tf_op jit(solution)/shard_map/ppermute | solution.py:45
  14.3 0.9 %setup.1 = (f32[45,256]{1,0:T(8,128)S(1)}, f32[32,256]{1,0:T(8,128)S(1)}, f32[32,256]{1,0:T(8,128)S(1)}) custom-call(f32[40,128]{1,0:T(8,128)S(1)} %packed_own.1.own_ref, f32[40,128]{1,0:T(8,128)S(1)} %collective-permute-done.below_ref, f32[40,128]{1,0:T(8,128)S(1)} %collective-permute-done.1.above_ref, f32[4,1024]{1,0:T(4,128)} %table_hbm.1), custom_call_target="tpu_custom_call" | custom-call | tf_op jit(solution)/shard_map/setup/pallas_call | solution.py:213
  15.2 1.1 %collective-permute-done.4 = f32[3,32,128]{2,1,0:T(8,128)S(1)} collective-permute-done((f32[3,32,128]{2,1,0:T(8,128)S(1)}, f32[3,32,128]{2,1,0:T(8,128)S(1)}, u32[]{:S(2)}, u32[]{:S(2)}) %collective-permute-start.4) | collective-permute-done | bytes 49184 | tf_op jit(solution)/shard_map/ppermute | solution.py:45
  16.4 0.2 collective-permute-start.6
  16.5 0.3 collective-permute-start.5
  16.9 0.9 %first_images.1.refs_7_.refs_4_ = f32[45,32,256]{2,1,0:T(8,128)S(1)} custom-call(bf16[2880,1440]{1,0:T(8,128)(2,1)S(1)} %split_piece.1.refs_0_, f32[32,256]{1,0:T(8,128)S(1)} %get-tuple-element.38.refs_1_.refs_6_.refs_8_.refs_3_), custom_call_target="tpu_custom_call" | custom-call | tf_op jit(solution)/shard_map/first_images/pallas_call | solution.py:260
  17.8 0.0 collective-permute-done.3.refs_3_
  17.8 0.0 collective-permute-done.2.refs_2_
  17.8 2.0 %early_columns.1 = (bf16[1440,512]{1,0:T(8,128)(2,1)S(1)}, bf16[2880,256]{1,0:T(8,128)(2,1)S(1)}, f32[45,32,256]{2,1,0:T(8,128)S(1)}) custom-call(bf16[2880,1440]{1,0:T(8,128)(2,1)S(1)} %split_piece.1.refs_0_, f32[3,32,128]{2,1,0:T(8,128)S(1)} %pad_maximum_fusion.refs_1_, f32[3,32,128]{2,1,0:T(8,128)S(1)} %collective-permute-done.2.refs_2_, ...), custom_call_target="tpu_custom_call" | custom-call | tf_op jit(solution)/shard_map/early_columns/pallas_call | solution.py:405
  19.8 0.0 collective-permute-done.6.refs_6_
  19.8 0.7 %collective-permute-done.5.refs_5_ = f32[1,3,32,128]{3,2,1,0:T(8,128)S(1)} collective-permute-done((f32[1,3,32,128]{3,2,1,0:T(8,128)S(1)}, f32[1,3,32,128]{3,2,1,0:T(8,128)S(1)}, u32[]{:S(2)}, u32[]{:S(2)}) %collective-permute-start.5) | collective-permute-done | bytes 49184 | tf_op jit(solution)/shard_map/ppermute | solution.py:45
  20.5 9.4 %shard_map.68 = (f32[10,32,128]{2,1,0:T(8,128)S(1)}, f32[10,32,128]{2,1,0:T(8,128)S(1)}, bf16[1440,512]{1,0:T(8,128)(2,1)S(1)}, bf16[2880,256]{1,0:T(8,128)(2,1)S(1)}) custom-call(bf16[2880,1440]{1,0:T(8,128)(2,1)S(1)} %split_piece.1.refs_0_, bf16[1440,512]{1,0:T(8,128)(2,1)S(1)} %get-tuple-element.39.refs_1_, ...), custom_call_target="tpu_custom_call" | custom-call | flops 6370099200 | bytes 1048576 | tf_op jit(solution)/shard_map/pallas_call | solution.py:558
  29.9 2.0 %shard_map.71 = (f32[10,32,128]{2,1,0:T(8,128)S(1)}, f32[5,32,128]{2,1,0:T(8,128)S(1)}, f32[10,32,128]{2,1,0:T(8,128)S(1)}, f32[5,32,128]{2,1,0:T(8,128)S(1)}) custom-call(bf16[2880,1440]{1,0:T(8,128)(2,1)S(1)} %split_piece.1.refs_0_, bf16[1440,512]{1,0:T(8,128)(2,1)S(1)} %get-tuple-element.43.refs_1_, bf16[2880,256]{1,0:T(8,128)(2,1)S(1)} %get-tuple-element.44.refs_2_, ...), custom_call_target="tpu_custom_call" | custom-call | flops 530841600 | bytes 1048576 | tf_op jit(solution)/shard_map/pallas_call | solution.py:558
  32.0 2.2 %shard_map.70 = (f32[10,32,128]{2,1,0:T(8,128)S(1)}, f32[5,32,128]{2,1,0:T(8,128)S(1)}, f32[10,32,128]{2,1,0:T(8,128)S(1)}, f32[5,32,128]{2,1,0:T(8,128)S(1)}) custom-call(bf16[2880,1440]{1,0:T(8,128)(2,1)S(1)} %split_piece.1.refs_0_, bf16[1440,512]{1,0:T(8,128)(2,1)S(1)} %get-tuple-element.43.refs_1_, bf16[2880,256]{1,0:T(8,128)(2,1)S(1)} %get-tuple-element.44.refs_2_, ...), custom_call_target="tpu_custom_call" | custom-call | flops 530841600 | bytes 1048576 | tf_op jit(solution)/shard_map/pallas_call | solution.py:558
  34.2 1.3 %collective-permute-start.8 = (f32[10,32,128]{2,1,0:T(8,128)S(1)}, f32[10,32,128]{2,1,0:T(8,128)S(1)}, u32[]{:S(2)}, u32[]{:S(2)}) collective-permute-start(f32[10,32,128]{2,1,0:T(8,128)S(1)} %get-tuple-element.55), channel_id=1, source_target_pairs={{0,16},{1,17},{2,18},{3,19},{4,20},{5,21},{6,22},{7,23},{8,24},{9,... | collective-permute-start | bytes 491528 | tf_op jit(solution)/shard_map/ppermute | solution.py:45
  35.5 0.7 %collective-permute-start.9 = (f32[10,32,128]{2,1,0:T(8,128)S(1)}, f32[10,32,128]{2,1,0:T(8,128)S(1)}, u32[]{:S(2)}, u32[]{:S(2)}) collective-permute-start(f32[10,32,128]{2,1,0:T(8,128)S(1)} %get-tuple-element.56), channel_id=1, source_target_pairs={{0,20},{1,21},{2,22},{3,23},{4,24},{5,25},{6,26},{7,27},{8,28},{9,... | collective-permute-start | bytes 491528 | tf_op jit(solution)/shard_map/ppermute | solution.py:45
  36.2 2.0 %collective-permute-start.7 = (f32[10,32,128]{2,1,0:T(8,128)S(1)}, f32[10,32,128]{2,1,0:T(8,128)S(1)}, u32[]{:S(2)}, u32[]{:S(2)}) collective-permute-start(f32[10,32,128]{2,1,0:T(8,128)S(1)} %get-tuple-element.54), channel_id=1, source_target_pairs={{0,28},{1,29},{2,30},{3,31},{4,16},{5,17},{6,18},{7,19},{8,20},{9,... | collective-permute-start | bytes 491528 | tf_op jit(solution)/shard_map/ppermute | solution.py:45
  38.2 0.0 collective-permute-start.11
  38.2 1.7 %collective-permute-start.10 = (f32[5,32,128]{2,1,0:T(8,128)S(1)}, f32[5,32,128]{2,1,0:T(8,128)S(1)}, u32[]{:S(2)}, u32[]{:S(2)}) collective-permute-start(f32[5,32,128]{2,1,0:T(8,128)S(1)} %get-tuple-element.57), channel_id=1, source_target_pairs={{0,12},{1,13},{2,14},{3,15},{4,0},{5,1},{6,2},{7,3},{8,4},{9,5},{1... | collective-permute-start | bytes 245768 | tf_op jit(solution)/shard_map/ppermute | solution.py:45
  39.9 1.2 %shard_map.69 = (f32[5,32,128]{2,1,0:T(8,128)S(1)}, f32[5,32,128]{2,1,0:T(8,128)S(1)}, f32[32,128]{1,0:T(8,128)S(1)}) custom-call(bf16[2880,1440]{1,0:T(8,128)(2,1)S(1)} %split_piece.1.refs_0_, bf16[1440,512]{1,0:T(8,128)(2,1)S(1)} %get-tuple-element.43.refs_1_, bf16[2880,256]{1,0:T(8,128)(2,1)S(1)} %get-tuple-element.44.refs_2_, ...), custom_call_target="tpu_custom_call" | custom-call | flops 530841600 | bytes 1048576 | tf_op jit(solution)/shard_map/pallas_call | solution.py:558
  41.2 0.9 %turned_tiles.1.refs_1_.refs_5_ = f32[45,32,128]{2,1,0:T(8,128)S(1)} custom-call(f32[10,32,128]{2,1,0:T(8,128)S(1)} %get-tuple-element.46.refs_0_, f32[10,32,128]{2,1,0:T(8,128)S(1)} %get-tuple-element.47.refs_1_, f32[10,32,128]{2,1,0:T(8,128)S(1)} %get-tuple-element.48.refs_2_, f32[5,32,128]{2,1,0:T(8,128)S(1)} %get-tuple-element.49.refs_3_, ...), custom_call_target="tpu_custom_call" | custom-call | flops 1048576 | bytes 2097152 | tf_op jit(solution)/shard_map/turned_tiles/pallas_call | solution.py:634
  42.1 0.7 %near_sums.1 = (f32[48,128]{1,0:T(8,128)S(1)}, f32[4,1024]{1,0:T(4,128)}) custom-call(f32[5,32,128]{2,1,0:T(8,128)S(1)} %get-tuple-element.45.refs_0_, f32[45,32,128]{2,1,0:T(8,128)S(1)} %turned_tiles.1.refs_1_.refs_5_, f32[32,128]{1,0:T(8,128)S(1)} %get-tuple-element.52.refs_2_), custom_call_target="tpu_custom_call" | custom-call | tf_op jit(solution)/shard_map/near_sums/pallas_call | solution.py:663
  42.8 0.5 %collective-permute-done.11.refs_4_ = f32[5,32,128]{2,1,0:T(8,128)S(1)} collective-permute-done((f32[5,32,128]{2,1,0:T(8,128)S(1)}, f32[5,32,128]{2,1,0:T(8,128)S(1)}, u32[]{:S(2)}, u32[]{:S(2)}) %collective-permute-start.11) | collective-permute-done | bytes 81952 | tf_op jit(solution)/shard_map/ppermute | solution.py:45
  43.3 0.0 collective-permute-done.10.refs_3_
  43.3 0.0 collective-permute-done.8.refs_1_
  43.3 0.3 collective-permute-done.9.refs_2_
  43.7 4.0 %collective-permute-done.7.refs_0_ = f32[10,32,128]{2,1,0:T(8,128)S(1)} collective-permute-done((f32[10,32,128]{2,1,0:T(8,128)S(1)}, f32[10,32,128]{2,1,0:T(8,128)S(1)}, u32[]{:S(2)}, u32[]{:S(2)}) %collective-permute-start.7) | collective-permute-done | bytes 163872 | tf_op jit(solution)/shard_map/ppermute | solution.py:45
  47.6 0.9 %total_sums.1 = f32[4,45]{1,0:T(4,128)} custom-call(f32[10,32,128]{2,1,0:T(8,128)S(1)} %collective-permute-done.7.refs_0_, f32[10,32,128]{2,1,0:T(8,128)S(1)} %collective-permute-done.8.refs_1_, f32[10,32,128]{2,1,0:T(8,128)S(1)} %collective-permute-done.9.refs_2_, f32[5,32,128]{2,1,0:T(8,128)S(1)} %collective-permute-done.10.refs_3_, ...), custom_call_target="tpu_custom_call" | custom-call | tf_op jit(solution)/shard_map/total_sums/pallas_call | solution.py:699
  (4 shorter events, 0.0 us)
Async XLA Ops:
  1.5 8.9 %collective-permute-start.1 = (f32[40,128]{1,0:T(8,128)S(1)}, f32[40,128]{1,0:T(8,128)S(1)}, u32[]{:S(2)}, u32[]{:S(2)}) collective-permute-start(f32[40,128]{1,0:T(8,128)S(1)} %packed_own.1.own_ref), channel_id=1, source_target_pairs={{0,3},{1,0},{2,1},{3,2},{4,7},{5,4},{6,5},{7,6},{8,11},{9,8},{10,9... | collective-permute-start | bytes 61448 | tf_op jit(solution)/shard_map/ppermute | solution.py:45
  6.6 5.6 %collective-permute-start = (f32[40,128]{1,0:T(8,128)S(1)}, f32[40,128]{1,0:T(8,128)S(1)}, u32[]{:S(2)}, u32[]{:S(2)}) collective-permute-start(f32[40,128]{1,0:T(8,128)S(1)} %packed_own.1.own_ref), channel_id=1, source_target_pairs={{0,1},{1,2},{2,3},{3,0},{4,5},{5,6},{6,7},{7,4},{8,9},{9,10},{10,1... | collective-permute-start | bytes 61448 | tf_op jit(solution)/shard_map/ppermute | solution.py:45
  12.2 4.1 %collective-permute-start.4 = (f32[3,32,128]{2,1,0:T(8,128)S(1)}, f32[3,32,128]{2,1,0:T(8,128)S(1)}, u32[]{:S(2)}, u32[]{:S(2)}) collective-permute-start(f32[3,32,128]{2,1,0:T(8,128)S(1)} %pad_maximum_fusion.refs_1_), channel_id=1, source_target_pairs={{0,16},{1,17},{2,18},{3,19},{4,20},{5,21},{6,22},{7,23},{8,24},{9,... | collective-permute-start | bytes 147464 | tf_op jit(solution)/shard_map/ppermute | solution.py:45
  13.8 4.0 %collective-permute-start.3 = (f32[3,32,128]{2,1,0:T(8,128)S(1)}, f32[3,32,128]{2,1,0:T(8,128)S(1)}, u32[]{:S(2)}, u32[]{:S(2)}) collective-permute-start(f32[3,32,128]{2,1,0:T(8,128)S(1)} %pad_maximum_fusion.refs_1_), channel_id=1, source_target_pairs={{0,12},{1,13},{2,14},{3,15},{4,0},{5,1},{6,2},{7,3},{8,4},{9,5},{1... | collective-permute-start | bytes 147464 | tf_op jit(solution)/shard_map/ppermute | solution.py:45
  13.8 4.0 %collective-permute-start.2 = (f32[3,32,128]{2,1,0:T(8,128)S(1)}, f32[3,32,128]{2,1,0:T(8,128)S(1)}, u32[]{:S(2)}, u32[]{:S(2)}) collective-permute-start(f32[3,32,128]{2,1,0:T(8,128)S(1)} %pad_maximum_fusion.refs_1_), channel_id=1, source_target_pairs={{0,4},{1,5},{2,6},{3,7},{4,8},{5,9},{6,10},{7,11},{8,12},{9,13},{1... | collective-permute-start | bytes 147464 | tf_op jit(solution)/shard_map/ppermute | solution.py:45
  16.4 3.4 %collective-permute-start.6 = (f32[1,3,32,128]{3,2,1,0:T(8,128)S(1)}, f32[1,3,32,128]{3,2,1,0:T(8,128)S(1)}, u32[]{:S(2)}, u32[]{:S(2)}) collective-permute-start(f32[1,3,32,128]{3,2,1,0:T(8,128)S(1)} %bitcast.13), channel_id=1, source_target_pairs={{0,12},{1,13},{2,14},{3,15},{4,0},{5,1},{6,2},{7,3},{8,4},{9,5},{1... | collective-permute-start | bytes 147464 | tf_op jit(solution)/shard_map/ppermute | solution.py:45
  16.5 4.0 %collective-permute-start.5 = (f32[1,3,32,128]{3,2,1,0:T(8,128)S(1)}, f32[1,3,32,128]{3,2,1,0:T(8,128)S(1)}, u32[]{:S(2)}, u32[]{:S(2)}) collective-permute-start(f32[1,3,32,128]{3,2,1,0:T(8,128)S(1)} %bitcast.14), channel_id=1, source_target_pairs={{0,4},{1,5},{2,6},{3,7},{4,8},{5,9},{6,10},{7,11},{8,12},{9,13},{1... | collective-permute-start | bytes 147464 | tf_op jit(solution)/shard_map/ppermute | solution.py:45
  34.2 9.1 %collective-permute-start.8 = (f32[10,32,128]{2,1,0:T(8,128)S(1)}, f32[10,32,128]{2,1,0:T(8,128)S(1)}, u32[]{:S(2)}, u32[]{:S(2)}) collective-permute-start(f32[10,32,128]{2,1,0:T(8,128)S(1)} %get-tuple-element.55), channel_id=1, source_target_pairs={{0,16},{1,17},{2,18},{3,19},{4,20},{5,21},{6,22},{7,23},{8,24},{9,... | collective-permute-start | bytes 491528 | tf_op jit(solution)/shard_map/ppermute | solution.py:45
  35.5 8.1 %collective-permute-start.9 = (f32[10,32,128]{2,1,0:T(8,128)S(1)}, f32[10,32,128]{2,1,0:T(8,128)S(1)}, u32[]{:S(2)}, u32[]{:S(2)}) collective-permute-start(f32[10,32,128]{2,1,0:T(8,128)S(1)} %get-tuple-element.56), channel_id=1, source_target_pairs={{0,20},{1,21},{2,22},{3,23},{4,24},{5,25},{6,26},{7,27},{8,28},{9,... | collective-permute-start | bytes 491528 | tf_op jit(solution)/shard_map/ppermute | solution.py:45
  36.2 11.4 %collective-permute-start.7 = (f32[10,32,128]{2,1,0:T(8,128)S(1)}, f32[10,32,128]{2,1,0:T(8,128)S(1)}, u32[]{:S(2)}, u32[]{:S(2)}) collective-permute-start(f32[10,32,128]{2,1,0:T(8,128)S(1)} %get-tuple-element.54), channel_id=1, source_target_pairs={{0,28},{1,29},{2,30},{3,31},{4,16},{5,17},{6,18},{7,19},{8,20},{9,... | collective-permute-start | bytes 491528 | tf_op jit(solution)/shard_map/ppermute | solution.py:45
  38.2 5.1 %collective-permute-start.11 = (f32[5,32,128]{2,1,0:T(8,128)S(1)}, f32[5,32,128]{2,1,0:T(8,128)S(1)}, u32[]{:S(2)}, u32[]{:S(2)}) collective-permute-start(f32[5,32,128]{2,1,0:T(8,128)S(1)} %get-tuple-element.58), channel_id=1, source_target_pairs={{0,4},{1,5},{2,6},{3,7},{4,8},{5,9},{6,10},{7,11},{8,12},{9,13},{1... | collective-permute-start | bytes 245768 | tf_op jit(solution)/shard_map/ppermute | solution.py:45
  38.2 5.1 %collective-permute-start.10 = (f32[5,32,128]{2,1,0:T(8,128)S(1)}, f32[5,32,128]{2,1,0:T(8,128)S(1)}, u32[]{:S(2)}, u32[]{:S(2)}) collective-permute-start(f32[5,32,128]{2,1,0:T(8,128)S(1)} %get-tuple-element.57), channel_id=1, source_target_pairs={{0,12},{1,13},{2,14},{3,15},{4,0},{5,1},{6,2},{7,3},{8,4},{9,5},{1... | collective-permute-start | bytes 245768 | tf_op jit(solution)/shard_map/ppermute | solution.py:45
